TPU v7x, 32 devices: a whole 2x2x4 slice. The times are simulated.
32 devices in a mesh: rows: 8 (over y, x, core), feat: 4 (over z).
Axes of the slice: x: 2, y: 2, z: 4, core: 2. Of those that a mesh axis runs over, the one named last changes fastest.
Arguments:
- features: bfloat16 [1536, 16384], P('rows', 'feat'), may hold values from -0.5 to 0.5
- labels: int32 [1536], P('rows'), may hold values 0 or 1
- posterior: bfloat16 [16384], P('feat'), may hold values from -1 to 1
- prior_prec: float32 [16384], P('feat'), may hold values from 1 to 10
Outputs:
- hessian: float32 [16384, 16384], P('feat', 'rows')
- gradient: float32 [16384], P('feat')
All inputs are finite; a program needn't handle non-finite values. No bound on the sum of `labels` on one device may be relied on, other than what follows from the above.
Results may differ from a plain program's by a relative error of at most 0.003.
Values may be sent and summed in bfloat16 or wider, within the bound.
A program may use at most 128 MiB of HBM per device.

v0:
```python
import jax
import jax.numpy as jnp
from jax import lax
from jax.sharding import PartitionSpec as P


def per_device(features, labels, posterior, prior_prec):
    row_count = lax.axis_size("rows")
    feat_count = lax.axis_size("feat")
    row_index = lax.axis_index("rows")
    feat_index = lax.axis_index("feat")
    block_width = features.shape[1]
    col_width = block_width * feat_count // row_count
    partial_value = jnp.dot(features, posterior, preferred_element_type=jnp.float32)
    margins = lax.psum(partial_value, "feat")
    chance = jax.nn.sigmoid(margins)
    weight = (chance * (1.0 - chance)).astype(jnp.bfloat16)
    residual = (labels.astype(jnp.float32) - chance).astype(jnp.bfloat16)
    all_rows, all_weight = (
        lax.all_gather(features, "rows", axis=0, tiled=True),
        lax.all_gather(weight, "rows", axis=0, tiled=True),
    )
    local_grad = jnp.dot(residual, features, preferred_element_type=jnp.float32)
    summed = lax.psum(local_grad, "rows")
    gradient = summed - prior_prec * posterior.astype(jnp.float32)
    full_width = lax.all_gather(features, "feat", axis=1, tiled=True)
    column_rows = lax.all_to_all(full_width, "rows", split_axis=1, concat_axis=0, tiled=True)
    weighted = all_weight[:, None] * all_rows
    product = lax.dot_general(
        weighted, column_rows, (((0,), (0,)), ((), ())), preferred_element_type=jnp.float32
    )
    global_rows = feat_index * block_width + jnp.arange(block_width, dtype=jnp.int32)
    global_cols = row_index * col_width + jnp.arange(col_width, dtype=jnp.int32)
    on_diagonal = global_rows[:, None] == global_cols[None, :]
    hessian = product + jnp.where(on_diagonal, prior_prec[:, None], jnp.float32(0.0))
    return (hessian, gradient)


def solution(mesh):
    in_specs = (P("rows", "feat"), P("rows"), P("feat"), P("feat"))
    out_specs = (P("feat", "rows"), P("feat"))
    return jax.shard_map(
        per_device, mesh=mesh, in_specs=in_specs, out_specs=out_specs, check_vma=False
    )
```

profile of v0, /device:TPU:9, one launch (start us, length us, event | category | flops | bytes accessed | tf_op | source)
XLA Modules:
  0.0 302.2 jit_solution(11984968131884465313)
XLA Ops:
  7.2 0.0 all-gather.5.cloned.1.call-start
  7.2 0.7 all-gather.5.cloned.1.call-update
  7.9 0.0 all-gather.3.cloned.1.call-start
  7.9 0.7 all-gather.3.cloned.1.call-update
  8.6 114.5 %all-gather.5.cloned.1.call-done = bf16[192,16384]{1,0:T(8,128)(2,1)} async-done(((bf16[192,4096]{1,0:T(8,128)(2,1)}), bf16[192,16384]{1,0:T(8,128)(2,1)}) %all-gather.5.cloned.1.call-update) | async-done | bytes 6291472 | tf_op jit(solution)/shard_map/all_gather | solution.py:26
  123.1 0.0 copy-start.1
  123.1 0.0 copy-start.3
  123.1 6.7 %copy.10 = bf16[24,8,8,2048]{3,2,0,1:T(8,128)(2,1)} copy(bf16[24,8,8,2048]{3,2,1,0:T(8,128)(2,1)} %bitcast.16) | data formatting | bytes 12582912 | tf_op jit(solution)/shard_map/all_to_all | solution.py:27
  129.9 5.3 %all-to-all-start = ((bf16[192,8,2048]{2,0,1:T(8,128)(2,1)}), bf16[192,8,2048]{2,0,1:T(8,128)(2,1)}, u32[]{:S(2)}, u32[]{:S(2)}) async-start(bf16[192,8,2048]{2,0,1:T(8,128)(2,1)} %bitcast.15), calls=%async_computation | async-start | bytes 12582912 | tf_op jit(solution)/shard_map/all_to_all | solution.py:27
  135.2 0.0 copy-done.1
  135.2 0.0 copy-done
  135.3 0.5 fusion.3
  135.8 10.2 %psum.14 = f32[192]{0:T(256)S(1)} all-reduce(f32[192]{0:T(256)S(1)} %bitcast.18), channel_id=1, replica_groups=mesh['rows'=8,'feat'=4] {'feat'}, use_global_device_ids=true, to_apply=%region_0.0 | all-reduce | flops 192 | bytes 1536 | tf_op jit(solution)/shard_map/psum | solution.py:15
  146.0 0.0 copy-done.3
  146.0 0.0 copy-done.4
  146.0 0.6 dynamic-slice
  147.3 0.2 dynamic-update-slice
  147.5 90.5 %all-reduce = bf16[1536]{0:T(1024)(128)(2,1)S(1)} all-reduce(bf16[1536]{0:T(1024)(128)(2,1)S(1)} %dynamic-update-slice), channel_id=1, replica_groups=mesh['rows'=8,'feat'=4] {'rows'}, use_global_device_ids=true, to_apply=%add | all-reduce | flops 1536 | bytes 6144
  238.1 0.3 fusion.4
  238.4 21.5 %psum.15 = f32[4096]{0:T(1024)S(1)} all-reduce(f32[4096]{0:T(1024)S(1)} %bitcast.17), channel_id=1, replica_groups=mesh['rows'=8,'feat'=4] {'rows'}, use_global_device_ids=true, to_apply=%region_1.0 | all-reduce | flops 4096 | bytes 32768 | tf_op jit(solution)/shard_map/psum | solution.py:24
  259.9 0.0 copy-done.2
  259.9 0.6 multiply_subtract_fusion
  260.5 0.0 all-to-all-done
  260.5 34.9 %select_add_fusion = f32[4096,2048]{1,0:T(8,128)} fusion(bf16[1536,2048]{1,0:T(8,128)(2,1)} %bitcast.3, f32[4096]{0:T(1024)S(1)} %copy-done.2, s32[2048]{0:T(1024)S(1)} %iota_add_fusion.1, s32[4096]{0:T(1024)S(1)} %iota_add_fusion, bf16[1536,4096]{1,0:T(8,128)(2,1)} %all-gather.3.cloned.1.call-done, bf16[1536]{0:T(1024)(128)(2,1)S(1)} %all-reduce), kind=kOutput, calls=%fused_computation | convolution fusion | flops 25801261056 | bytes 52472832 | tf_op jit(solution)/shard_map/dot_general | solution.py:29
  (11 shorter events, 0.1 us)
Async XLA Ops:
  7.2 116.0 %all-gather.5.cloned.1.call-start = ((), (), s32[]{:S(2)}) async-start(), calls=%async_computation.2 | async-start | bytes 7864320 | tf_op jit(solution)/shard_map/all_gather | solution.py:26
  7.9 252.6 %all-gather.3.cloned.1.call-start = ((), (), s32[]{:S(2)}) async-start(), calls=%async_computation.1 | async-start | bytes 14155776 | tf_op jit(solution)/shard_map/all_gather | solution.py:20
  123.1 12.1 %copy-start.1 = (bf16[4096]{0:T(1024)(128)(2,1)S(1)}, bf16[4096]{0:T(1024)(128)(2,1)}, u32[]{:S(2)}) copy-start(bf16[4096]{0:T(1024)(128)(2,1)} %param.6) | copy-start | bytes 24580
  123.1 12.1 %copy-start = (bf16[192,4096]{1,0:T(8,128)(2,1)S(1)}, bf16[192,4096]{1,0:T(8,128)(2,1)}, u32[]{:S(2)}) copy-start(bf16[192,4096]{1,0:T(8,128)(2,1)} %param.4) | copy-start | bytes 4718596
  123.1 22.9 %copy-start.3 = (s32[192]{0:T(256)S(1)}, s32[192]{0:T(256)}, u32[]{:S(2)}) copy-start(s32[192]{0:T(256)} %param.5) | copy-start | bytes 2308
  123.1 22.9 %copy-start.4 = (u32[32]{0:T(128)S(1)}, u32[32]{0:T(128)}, u32[]{:S(2)}) copy-start(u32[32]{0:T(128)} %constant.19) | copy-start | bytes 388
  123.1 136.7 %copy-start.2 = (f32[4096]{0:T(1024)S(1)}, f32[4096]{0:T(1024)}, u32[]{:S(2)}) copy-start(f32[4096]{0:T(1024)} %param.7) | copy-start | bytes 49156
  129.9 130.6 %all-to-all-start = ((bf16[192,8,2048]{2,0,1:T(8,128)(2,1)}), bf16[192,8,2048]{2,0,1:T(8,128)(2,1)}, u32[]{:S(2)}, u32[]{:S(2)}) async-start(bf16[192,8,2048]{2,0,1:T(8,128)(2,1)} %bitcast.15), calls=%async_computation | async-start | bytes 12582912 | tf_op jit(solution)/shard_map/all_to_all | solution.py:27
Sparse Core Ops, SparseCore 0:
  9.5 113.5 all-gather.4
  125.0 134.1 all-gather.2
where the time goes:
time: 307 us; the launch traced here: 302 us
  blocking collectives  122 us (40%)
  waiting for transfers between devices  116 us (38%)
  matrix products  35.7 us (12%)
  between operations  14.8 us (5%)
  local copies, waits for them, and re-layouts  7.61 us (2%)
  starting transfers between devices  5.42 us (2%)
    all_gather x1, waiting for transfers between devices, per_device(): full_width = lax.all_gather(features, 'feat', axis=1, tiled=True)  114 us
    unnamed x1, blocking collectives  90.5 us
    dot_general x1, matrix products, per_device(): lax.dot_general(weighted, column_rows, (((0,), (0,)), ((), ())), preferre...  34.9 us
    psum x1, blocking collectives, per_device(): summed = lax.psum(local_grad, 'rows')  21.5 us
    psum x1, blocking collectives, per_device(): margins = lax.psum(partial_value, 'feat')  10.2 us
    all_to_all x1, local copies, waits for them, and re-layouts, per_device(): lax.all_to_all(full_width, 'rows', split_axis=1, concat_axis=0, tiled=True)  6.73 us
  transfers between devices with their start and end apart: 3, of which 1 were waited for; matrix products, arithmetic and copies ran while one was open for 3% of the time, Pallas kernels for 0%

commit v1 on v0

v1 whole, which is shorter than its diff:
```python
import functools

import jax
import jax.numpy as jnp
from jax import lax
from jax.experimental import pallas as pl
from jax.experimental.pallas import tpu as pltpu
from jax.sharding import PartitionSpec as P

MESH = pl.DeviceIdType.MESH
SPLIT = 2


def gather_kernel(
    row_count, feat_count, x_ref, st_ref, all_ref, col_ref, stat_ref,
    ring, zs, zr, ps, pr, ds, dr, cs, cr, cl, ss, sr, ts, tr, lsem,
):
    r = lax.axis_index("rows")
    f = lax.axis_index("feat")
    n, width = x_ref.shape
    half = width // 2
    col_width = col_ref.shape[1]
    unit = min(col_width, half)
    per_half = half // unit
    per_owner = col_width // unit
    chips = row_count // 2
    bits = chips.bit_length() - 1
    part = n // SPLIT

    def rows_of(device):
        return pl.ds(pl.multiple_of(device * n, n), n)

    def remote(src, dst, send, recv, **where):
        return pltpu.make_async_remote_copy(
            src_ref=src, dst_ref=dst, send_sem=send, recv_sem=recv,
            device_id=where, device_id_type=MESH,
        )

    sends = []

    def go(copy):
        copy.start()
        sends.append(copy)

    def ring_slice(step, h, k):
        rows, cols = pl.ds(k * part, part), pl.ds(h * half, half)
        return x_ref.at[rows, cols] if step == 0 else ring.at[step - 1, rows, cols]

    def ring_copy(step, h, k):
        to = lax.rem(f + (1 if h == 0 else feat_count - 1), feat_count)
        return remote(
            ring_slice(step, h, k),
            ring.at[step, pl.ds(k * part, part), pl.ds(h * half, half)],
            zs.at[step, h, k], zr.at[step, h, k], feat=to,
        )

    def column_sends(step, h, k, start):
        block = lax.rem(f + (feat_count - step if h == 0 else step), feat_count)
        for u in range(per_half):
            inner = h * half + u * unit
            if width % col_width == 0:
                owner = block * (width // col_width) + inner // col_width
                offset = inner % col_width
                slot = offset // unit
            else:
                owner = (block * width + inner) // col_width
                slot = ((block * width + inner) % col_width) // unit
                offset = pl.multiple_of(slot * unit, unit)
            src = ring_slice(step, h, k).at[:, pl.ds(u * unit, unit)]
            dst = col_ref.at[
                pl.ds(pl.multiple_of(r * n + k * part, part), part), pl.ds(offset, unit)
            ]
            send = cs.at[step, h, k, u]

            @pl.when(owner != r)
            def _():
                copy = remote(src, dst, send, cr.at[r, slot, k], rows=owner)
                copy.start() if start else copy.wait_send()

            if start:
                @pl.when(owner == r)
                def _():
                    pltpu.make_async_copy(src, dst, cl.at[slot, k]).start()

    def order(h):
        return list(range(bits)) if h == 0 else list(range(bits))[::-1]

    def spread(h, stage, mask):
        bit = 1 << order(h)[stage]
        origin = r ^ (2 * mask)
        cols = pl.ds(h * half, half)
        src = x_ref.at[:, cols] if mask == 0 else all_ref.at[rows_of(origin), cols]
        return remote(
            src, all_ref.at[rows_of(origin), cols],
            ps.at[h, mask | bit], pr.at[h, mask | bit], rows=r ^ (2 * bit),
        )

    def partner(h, mask):
        origin = r ^ (2 * mask)
        cols = pl.ds(h * half, half)
        src = x_ref.at[:, cols] if mask == 0 else all_ref.at[rows_of(origin), cols]
        return remote(
            src, all_ref.at[rows_of(origin), cols],
            ds.at[h, mask], dr.at[h, mask], rows=r ^ 1,
        )

    def masks_before(h, stage):
        found = [0]
        for b in order(h)[:stage]:
            found += [m | (1 << b) for m in found]
        return found

    for k in range(SPLIT):
        for h in range(2):
            go(ring_copy(0, h, k))
    stat_local = pltpu.make_async_copy(st_ref, stat_ref.at[r, f], lsem.at[0])
    stat_local.start()
    for d in range(1, feat_count):
        go(remote(
            st_ref, stat_ref.at[r, f], ss.at[d], sr.at[d],
            feat=lax.rem(f + d, feat_count),
        ))
    for stage in range(bits):
        for h in range(2):
            go(spread(h, stage, 0))
    for h in range(2):
        go(partner(h, 0))
    own = pltpu.make_async_copy(x_ref, all_ref.at[rows_of(r)], lsem.at[1])
    own.start()
    for k in range(SPLIT):
        for h in range(2):
            column_sends(0, h, k, True)

    stat_local.wait()
    for d in range(1, feat_count):
        remote(
            st_ref, stat_ref.at[r, lax.rem(f + feat_count - d, feat_count)],
            ss.at[d], sr.at[d], feat=f,
        ).wait_recv()
    for d in range(1, row_count):
        go(remote(
            stat_ref.at[r], stat_ref.at[r], ts.at[d], tr.at[d],
            rows=lax.rem(r + d, row_count),
        ))

    def relay(stage):
        for h in range(2):
            bit = 1 << order(h)[stage]
            for m in masks_before(h, stage):
                mask = m | bit
                cols = pl.ds(h * half, half)
                remote(
                    x_ref.at[:, cols], all_ref.at[rows_of(r ^ (2 * mask)), cols],
                    ps.at[h, mask], pr.at[h, mask], rows=r,
                ).wait_recv()
                for later in range(stage + 1, bits):
                    go(spread(h, later, mask))
                go(partner(h, mask))

    for step in range(1, feat_count):
        for k in range(SPLIT):
            for h in range(2):
                ring_copy(step - 1, h, k).wait_recv()
                if step < feat_count - 1:
                    go(ring_copy(step, h, k))
                column_sends(step, h, k, True)
        if step <= bits:
            relay(step - 1)
    for stage in range(feat_count - 1, bits):
        relay(stage)

    for h in range(2):
        for mask in range(chips):
            cols = pl.ds(h * half, half)
            remote(
                x_ref.at[:, cols], all_ref.at[rows_of(r ^ (2 * mask) ^ 1), cols],
                ds.at[h, mask], dr.at[h, mask], rows=r,
            ).wait_recv()
    for d in range(1, row_count):
        origin = lax.rem(r + row_count - d, row_count)
        remote(
            stat_ref.at[origin], stat_ref.at[origin], ts.at[d], tr.at[d], rows=r
        ).wait_recv()
        for slot in range(per_owner):
            for k in range(SPLIT):
                dst = col_ref.at[
                    pl.ds(pl.multiple_of(origin * n + k * part, part), part),
                    pl.ds(slot * unit, unit),
                ]
                remote(
                    x_ref.at[pl.ds(0, part), pl.ds(0, unit)], dst,
                    cs.at[0, 0, 0, 0], cr.at[origin, slot, k], rows=r,
                ).wait_recv()
    for slot in range(per_owner):
        for k in range(SPLIT):
            dst = col_ref.at[
                pl.ds(pl.multiple_of(r * n + k * part, part), part),
                pl.ds(slot * unit, unit),
            ]
            pltpu.make_async_copy(
                x_ref.at[pl.ds(0, part), pl.ds(0, unit)], dst, cl.at[slot, k]
            ).wait()
    own.wait()
    for copy in sends:
        copy.wait_send()
    for step in range(feat_count):
        for k in range(SPLIT):
            for h in range(2):
                column_sends(step, h, k, False)


def gather(features, stats):
    row_count = lax.axis_size("rows")
    feat_count = lax.axis_size("feat")
    n, width = features.shape
    half = width // 2
    col_width = width * feat_count // row_count
    unit = min(col_width, half)
    chips = row_count // 2
    dma = pltpu.SemaphoreType.DMA
    return pl.pallas_call(
        functools.partial(gather_kernel, row_count, feat_count),
        out_shape=(
            jax.ShapeDtypeStruct((row_count * n, width), features.dtype),
            jax.ShapeDtypeStruct((row_count * n, col_width), features.dtype),
            jax.ShapeDtypeStruct((row_count, feat_count) + stats.shape, stats.dtype),
        ),
        in_specs=[pl.BlockSpec(memory_space=pltpu.VMEM)] * 2,
        out_specs=[pl.BlockSpec(memory_space=pl.ANY)] * 3,
        scratch_shapes=[
            pltpu.VMEM((feat_count - 1, n, width), features.dtype),
            dma((feat_count - 1, 2, SPLIT)), dma((feat_count - 1, 2, SPLIT)),
            dma((2, chips)), dma((2, chips)),
            dma((2, chips)), dma((2, chips)),
            dma((feat_count, 2, SPLIT, half // unit)),
            dma((row_count, col_width // unit, SPLIT)),
            dma((col_width // unit, SPLIT)),
            dma((feat_count,)), dma((feat_count,)),
            dma((row_count,)), dma((row_count,)),
            dma((2,)),
        ],
        compiler_params=pltpu.CompilerParams(
            has_side_effects=True, vmem_limit_bytes=32 * 1024 * 1024
        ),
        name="gather",
    )(features, stats)


def per_device(features, labels, posterior, prior_prec):
    row_count = lax.axis_size("rows")
    feat_count = lax.axis_size("feat")
    row_index = lax.axis_index("rows")
    feat_index = lax.axis_index("feat")
    n, block_width = features.shape
    col_width = block_width * feat_count // row_count
    partial_value = jnp.dot(features, posterior, preferred_element_type=jnp.float32)
    padded = -(-n // 512) * 512
    stats = jnp.concatenate([
        jnp.pad(partial_value, (0, padded - n)),
        jnp.pad(labels.astype(jnp.float32), (0, padded - n)),
    ]).reshape(-1, 128)
    all_rows, column_rows, all_stats = gather(features, stats)
    all_stats = all_stats.reshape(row_count, feat_count, 2, padded)[..., :n]
    margins = jnp.sum(all_stats[:, :, 0], axis=1).reshape(-1)
    all_labels = all_stats[:, 0, 1].reshape(-1)
    chance = jax.nn.sigmoid(margins)
    weight = (chance * (1.0 - chance)).astype(jnp.bfloat16)
    residual = (all_labels - chance).astype(jnp.bfloat16)
    summed = jnp.dot(residual, all_rows, preferred_element_type=jnp.float32)
    gradient = summed - prior_prec * posterior.astype(jnp.float32)
    weighted = weight[:, None] * all_rows
    product = lax.dot_general(
        weighted, column_rows, (((0,), (0,)), ((), ())), preferred_element_type=jnp.float32
    )
    global_rows = feat_index * block_width + jnp.arange(block_width, dtype=jnp.int32)
    global_cols = row_index * col_width + jnp.arange(col_width, dtype=jnp.int32)
    on_diagonal = global_rows[:, None] == global_cols[None, :]
    hessian = product + jnp.where(on_diagonal, prior_prec[:, None], jnp.float32(0.0))
    return (hessian, gradient)


def solution(mesh):
    in_specs = (P("rows", "feat"), P("rows"), P("feat"), P("feat"))
    out_specs = (P("feat", "rows"), P("feat"))
    return jax.shard_map(
        per_device, mesh=mesh, in_specs=in_specs, out_specs=out_specs, check_vma=False
    )
```

time: 307 us -> 215 us (0.70); the launches traced: 302 us -> 215 us
  Pallas kernels: 0 us -> 164 us
  blocking collectives: 122 us -> 0 us
  waiting for transfers between devices: 116 us -> 0 us
  between operations: 14.8 us -> 0.72 us
  starting transfers between devices: 5.42 us -> 0 us
    pallas_call x0 -> x1, Pallas kernels: none -> 164 us  [gather(): pl.pallas_call(functools.partial(gather_kernel, row_count, feat_count), o...]
    all_gather x2 -> x0, waiting for transfers between devices: 114 us -> none  [the longest x1 114 us: per_device(): full_width = lax.all_gather(features, 'feat', axis=1, tiled=True)]
    unnamed x1 -> x0, blocking collectives: 90.5 us -> none
    psum x2 -> x0, blocking collectives: 31.7 us -> none  [the longest x1 21.5 us: per_device(): summed = lax.psum(local_grad, 'rows')]
    unnamed x14 -> x13, local copies, waits for them, and re-layouts: 0.87 us -> 9.25 us
    all_to_all x1 -> x0, local copies, waits for them, and re-layouts: 6.73 us -> none  [per_device(): lax.all_to_all(full_width, 'rows', split_axis=1, concat_axis=0, tiled=True)]
    all_to_all x1 -> x0, starting transfers between devices: 5.34 us -> none  [per_device(): lax.all_to_all(full_width, 'rows', split_axis=1, concat_axis=0, tiled=True)]
  transfers between devices with their start and end apart: 3 -> 0, of which waited for: 1 -> 0; matrix products, arithmetic and copies ran while one was open for 3% -> 0% of each run, Pallas kernels for 0% -> 0%
where the time goes in v1:
time: 215 us
  Pallas kernels  164 us (76%)
  matrix products  38.7 us (18%)
  local copies, waits for them, and re-layouts  9.5 us (4%)
    pallas_call x1, Pallas kernels, gather(): pl.pallas_call(functools.partial(gather_kernel, row_count, feat_count), o...  164 us
    dot_general x1, matrix products, per_device(): lax.dot_general(weighted, column_rows, (((0,), (0,)), ((), ())), preferre...  35.1 us
    unnamed x13, local copies, waits for them, and re-layouts  9.25 us

profile of v1, /device:TPU:9, one launch (start us, length us, event | category | flops | bytes accessed | tf_op | source)
XLA Modules:
  0.0 214.8 jit_solution(1005749896341196002)
XLA Ops:
  0.6 0.7 reshape.38
  1.3 1.9 fusion.3
  3.3 0.7 convert_element_type.19
  4.0 0.0 copy-start.2
  4.0 1.4 copy-done.2
  5.4 164.4 %gather.1 = (bf16[1536,4096]{1,0:T(8,128)(2,1)S(1)}, bf16[1536,2048]{1,0:T(8,128)(2,1)S(1)}, f32[8,4,8,128]{3,2,1,0:T(8,128)S(1)}) custom-call(bf16[192,4096]{1,0:T(8,128)(2,1)S(1)} %copy-done.2, f32[8,128]{1,0:T(8,128)S(1)} %pad_maximum_fusion.st_ref), custom_call_target="tpu_custom_call" | custom-call | tf_op jit(solution)/shard_map/gather/pallas_call | solution.py:221
  169.8 0.0 copy-start
  169.8 4.5 %copy-done = bf16[1536,4096]{1,0:T(8,128)(2,1)} copy-done((bf16[1536,4096]{1,0:T(8,128)(2,1)}, bf16[1536,4096]{1,0:T(8,128)(2,1)S(1)}, u32[]{:S(2)}) %copy-start) | copy-done | bytes 12582936
  174.4 0.0 copy-start.3
  174.4 2.6 %copy-done.3 = bf16[1536,2048]{1,0:T(8,128)(2,1)} copy-done((bf16[1536,2048]{1,0:T(8,128)(2,1)}, bf16[1536,2048]{1,0:T(8,128)(2,1)S(1)}, u32[]{:S(2)}) %copy-start.3) | copy-done | bytes 6291480
  176.9 0.1 reshape.37
  177.1 0.1 div.11
  177.2 0.1 reshape_squeeze.3
  177.3 0.0 copy-start.1
  177.3 35.1 %select_add_fusion = f32[4096,2048]{1,0:T(8,128)} fusion(bf16[1536,2048]{1,0:T(8,128)(2,1)} %copy-done.3, f32[4096]{0:T(1024)} %param.7, s32[2048]{0:T(1024)S(1)} %iota_add_fusion.1, s32[4096]{0:T(1024)S(1)} %iota_add_fusion, bf16[1536,4096]{1,0:T(8,128)(2,1)} %copy-done, bf16[1536]{0:T(1024)(128)(2,1)S(1)} %get-tuple-element.9), kind=kOutput, calls=%fused_computation | convolution fusion | flops 25801261056 | bytes 52472832 | tf_op jit(solution)/shard_map/dot_general | solution.py:272
  212.4 0.0 copy-start.4
  212.4 0.0 copy-start.5
  212.4 0.0 copy-done.1
  212.4 1.7 fusion.4
  214.1 0.0 copy-done.4
  214.1 0.0 copy-done.5
  214.1 0.6 multiply_subtract_fusion
  (9 shorter events, 0.1 us)
Async XLA Ops:
  4.0 1.4 copy-start.2
  169.8 4.6 %copy-start = (bf16[1536,4096]{1,0:T(8,128)(2,1)}, bf16[1536,4096]{1,0:T(8,128)(2,1)S(1)}, u32[]{:S(2)}) copy-start(bf16[1536,4096]{1,0:T(8,128)(2,1)S(1)} %get-tuple-element.6) | copy-start | bytes 37748740
  174.4 2.6 %copy-start.3 = (bf16[1536,2048]{1,0:T(8,128)(2,1)}, bf16[1536,2048]{1,0:T(8,128)(2,1)S(1)}, u32[]{:S(2)}) copy-start(bf16[1536,2048]{1,0:T(8,128)(2,1)S(1)} %get-tuple-element.7) | copy-start | bytes 18874372
  177.3 35.1 %copy-start.1 = (bf16[1536,4096]{1,0:T(8,128)(2,1)S(1)}, bf16[1536,4096]{1,0:T(8,128)(2,1)}, u32[]{:S(2)}) copy-start(bf16[1536,4096]{1,0:T(8,128)(2,1)} %copy-done) | copy-start | bytes 37748740
  212.4 1.8 copy-start.4
  212.4 1.8 copy-start.5

commit v2 on v1

--- a/solution.py
+++ b/solution.py
@@ -8,7 +8,7 @@
 from jax.sharding import PartitionSpec as P
 
 MESH = pl.DeviceIdType.MESH
-SPLIT = 2
+SPLIT = 4
 
 
 def gather_kernel(

time: 215 us -> 216 us (level)
  no operation moved by 1% of the time
where the time goes in v2:
time: 216 us; the launch traced here: 215 us
  Pallas kernels  165 us (76%)
  matrix products  38.7 us (18%)
  local copies, waits for them, and re-layouts  9.5 us (4%)
    pallas_call x1, Pallas kernels, gather(): pl.pallas_call(functools.partial(gather_kernel, row_count, feat_count), o...  165 us
    dot_general x1, matrix products, per_device(): lax.dot_general(weighted, column_rows, (((0,), (0,)), ((), ())), preferre...  35.1 us
    unnamed x13, local copies, waits for them, and re-layouts  9.25 us

profile of v2, /device:TPU:9, one launch (start us, length us, event | category | flops | bytes accessed | tf_op | source)
XLA Modules:
  0.0 215.3 jit_solution(6579025364300996679)
XLA Ops:
  0.6 0.7 reshape.38
  1.3 1.9 fusion.3
  3.3 0.7 convert_element_type.19
  4.0 0.0 copy-start.2
  4.0 1.4 copy-done.2
  5.4 165.0 %gather.1 = (bf16[1536,4096]{1,0:T(8,128)(2,1)S(1)}, bf16[1536,2048]{1,0:T(8,128)(2,1)S(1)}, f32[8,4,8,128]{3,2,1,0:T(8,128)S(1)}) custom-call(bf16[192,4096]{1,0:T(8,128)(2,1)S(1)} %copy-done.2, f32[8,128]{1,0:T(8,128)S(1)} %pad_maximum_fusion.st_ref), custom_call_target="tpu_custom_call" | custom-call | tf_op jit(solution)/shard_map/gather/pallas_call | solution.py:221
  170.4 0.0 copy-start
  170.4 4.5 %copy-done = bf16[1536,4096]{1,0:T(8,128)(2,1)} copy-done((bf16[1536,4096]{1,0:T(8,128)(2,1)}, bf16[1536,4096]{1,0:T(8,128)(2,1)S(1)}, u32[]{:S(2)}) %copy-start) | copy-done | bytes 12582936
  174.9 0.0 copy-start.3
  174.9 2.6 %copy-done.3 = bf16[1536,2048]{1,0:T(8,128)(2,1)} copy-done((bf16[1536,2048]{1,0:T(8,128)(2,1)}, bf16[1536,2048]{1,0:T(8,128)(2,1)S(1)}, u32[]{:S(2)}) %copy-start.3) | copy-done | bytes 6291480
  177.5 0.1 reshape.37
  177.6 0.1 div.11
  177.7 0.1 reshape_squeeze.3
  177.8 0.0 copy-start.1
  177.9 35.1 %select_add_fusion = f32[4096,2048]{1,0:T(8,128)} fusion(bf16[1536,2048]{1,0:T(8,128)(2,1)} %copy-done.3, f32[4096]{0:T(1024)} %param.7, s32[2048]{0:T(1024)S(1)} %iota_add_fusion.1, s32[4096]{0:T(1024)S(1)} %iota_add_fusion, bf16[1536,4096]{1,0:T(8,128)(2,1)} %copy-done, bf16[1536]{0:T(1024)(128)(2,1)S(1)} %get-tuple-element.9), kind=kOutput, calls=%fused_computation | convolution fusion | flops 25801261056 | bytes 52472832 | tf_op jit(solution)/shard_map/dot_general | solution.py:272
  212.9 0.0 copy-start.4
  212.9 0.0 copy-start.5
  213.0 0.0 copy-done.1
  213.0 1.7 fusion.4
  214.7 0.0 copy-done.4
  214.7 0.0 copy-done.5
  214.7 0.6 multiply_subtract_fusion
  (9 shorter events, 0.1 us)
Async XLA Ops:
  4.0 1.4 copy-start.2
  170.4 4.6 %copy-start = (bf16[1536,4096]{1,0:T(8,128)(2,1)}, bf16[1536,4096]{1,0:T(8,128)(2,1)S(1)}, u32[]{:S(2)}) copy-start(bf16[1536,4096]{1,0:T(8,128)(2,1)S(1)} %get-tuple-element.6) | copy-start | bytes 37748740
  174.9 2.6 %copy-start.3 = (bf16[1536,2048]{1,0:T(8,128)(2,1)}, bf16[1536,2048]{1,0:T(8,128)(2,1)S(1)}, u32[]{:S(2)}) copy-start(bf16[1536,2048]{1,0:T(8,128)(2,1)S(1)} %get-tuple-element.7) | copy-start | bytes 18874372
  177.8 35.1 %copy-start.1 = (bf16[1536,4096]{1,0:T(8,128)(2,1)S(1)}, bf16[1536,4096]{1,0:T(8,128)(2,1)}, u32[]{:S(2)}) copy-start(bf16[1536,4096]{1,0:T(8,128)(2,1)} %copy-done) | copy-start | bytes 37748740
  212.9 1.8 copy-start.4
  212.9 1.8 copy-start.5
